TPU v7x, 32 devices: a whole 2x2x4 slice. The times are simulated.
32 devices in a mesh: occ: 4 (over z), vir: 8 (over y, x, core).
Axes of the slice: x: 2, y: 2, z: 4, core: 2. Of those that a mesh axis runs over, the one named last changes fastest.
Arguments:
- amplitudes: bfloat16 [352, 4096], P('occ', 'vir'), may hold values from -6 to 6
- integrals: bfloat16 [4096, 4096], P('vir', 'occ'), may hold values from -0.375 to 0.375
- labels: int32 [32], replicated, may hold values from 0 to 7
- slot_tile: int32 [32], replicated, may hold values from 0 to 31, each once
Outputs:
- residual: float32 [352, 4096], P(None, ('occ', 'vir'))
Inputs may be any that keep to these rules, and one draw needn't show every extreme that they name: `slot_tile`: each tile appears in exactly one slot.
All inputs are finite; a program needn't handle non-finite values.
Results may differ from a plain program's by a relative error of at most 0.0003.
Values may be sent and summed in bfloat16 or wider, within the bound.
No kernel may reach another device: no remote copies, remote signals or barrier semaphores. Data moves between devices by JAX's collectives and lax.ppermute only.
A program may use at most 128 MiB of HBM per device.

v0:
```python
import jax
import jax.numpy as jnp
from jax import lax
from jax.sharding import PartitionSpec as P

TILE = 128


def shards(amplitudes, integrals, labels, slot_tile):
    vir_index = lax.axis_index("vir")
    occ_index = lax.axis_index("occ")
    local_slots = integrals.shape[0] // TILE
    ab_tiles = integrals.shape[1] // TILE
    my_slots = lax.dynamic_slice_in_dim(slot_tile, vir_index * local_slots, local_slots)
    slot_label = labels[my_slots]
    ab_label = lax.dynamic_slice_in_dim(labels, occ_index * ab_tiles, ab_tiles)
    keep = (slot_label[:, None] == ab_label[None, :]).astype(jnp.bfloat16)
    keep_full = jnp.repeat(jnp.repeat(keep, TILE, axis=0), TILE, axis=1)
    masked = integrals * keep_full
    gathered = lax.all_gather(amplitudes, "occ", axis=0, tiled=True)
    summed = lax.psum_scatter(
        lax.dot_general(
            masked, gathered, (((0,), (1,)), ((), ())), preferred_element_type=jnp.float32
        ),
        "vir",
        scatter_dimension=0,
        tiled=True,
    )
    return jnp.transpose(summed)


def solution(mesh):
    in_specs = (P("occ", "vir"), P("vir", "occ"), P(), P())
    out_specs = P(None, ("occ", "vir"))
    return jax.shard_map(shards, mesh=mesh, in_specs=in_specs, out_specs=out_specs, check_vma=False)
```

profile of v0, /device:TPU:0, one launch (start us, length us, event | category | flops | bytes accessed | tf_op | source)
XLA Modules:
  0.0 74.6 jit_solution(17714155258452050967)
XLA Ops:
  6.5 0.0 copy-start
  6.5 0.0 reduce-scatter.2.cloned.1.call-start
  6.5 0.8 %compare_select_fusion = s32[4]{0:T(128)S(1)} fusion(s32[32]{0:T(128)} %param.7, s32[]{:T(128)S(6)} %select_n.9), kind=kLoop, calls=%fused_computation.5 | loop fusion | flops 12 | bytes 36 | tf_op jit(solution)/shard_map/select_n | solution.py:15
  7.4 0.7 dynamic_slice.7
  8.1 1.3 %gather_fusion = s32[4]{0:T(128)S(1)} fusion(s32[32]{0:T(128)} %param.6, s32[1024]{0:T(1024)S(1)} %pad_clamp_fusion), kind=kCustom, calls=%fused_computation | custom fusion | bytes 48 | tf_op jit(solution)/shard_map/gather | solution.py:15
  9.4 16.3 %all_gather.3 = bf16[352,512]{1,0:T(8,128)(2,1)S(1)} all-gather(bf16[88,512]{1,0:T(8,128)(2,1)} %param.4), channel_id=1, replica_groups=mesh['occ'=4,'vir'=8] {'occ'}, dimensions={0}, use_global_device_ids=true | all-gather | bytes 450560 | tf_op jit(solution)/shard_map/all_gather | solution.py:20
  25.7 0.1 compare_convert_fusion
  25.8 0.6 broadcast_in_dim.13
  26.4 0.0 copy-done
  26.4 1.7 %fusion = f32[1024,352]{0,1:T(8,128)} fusion(bf16[352,512]{1,0:T(8,128)(2,1)S(1)} %all_gather.3, bf16[512,1024]{1,0:T(8,128)(2,1)S(1)} %copy-done, bf16[64,8,8,128]{3,2,1,0:T(8,128)(2,1)S(1)} %bitcast.7), kind=kOutput, calls=%fused_computation.2 | convolution fusion | flops 369623040 | bytes 3899392 | tf_op jit(solution)/shard_map/dot_general | solution.py:22
  28.1 0.0 reduce-scatter.2.cloned.1.call-update
  28.1 39.7 %reduce-scatter.2.cloned.1.call-done = f32[128,352]{0,1:T(8,128)} async-done(((f32[1024,352]{0,1:T(8,128)}), f32[128,352]{0,1:T(8,128)}) %reduce-scatter.2.cloned.1.call-update) | async-done | bytes 180240 | tf_op jit(solution)/shard_map/reduce_scatter | solution.py:21
  (2 shorter events, 0.0 us)
Async XLA Ops:
  6.5 19.8 %copy-start = (bf16[512,1024]{1,0:T(8,128)(2,1)S(1)}, bf16[512,1024]{1,0:T(8,128)(2,1)}, u32[]{:S(2)}) copy-start(bf16[512,1024]{1,0:T(8,128)(2,1)} %param.5) | copy-start | bytes 3145732
  6.5 61.2 %reduce-scatter.2.cloned.1.call-start = ((), (), s32[]{:S(2)}) async-start(), calls=%async_computation.1 | async-start | bytes 1622016 | tf_op jit(solution)/shard_map/reduce_scatter | solution.py:21
Sparse Core Ops, SparseCore 0:
  28.2 39.5 reduce-scatter.1
where the time goes:
time: 74.8 us; the launch traced here: 74.6 us
  waiting for transfers between devices  39.7 us (53%)
  blocking collectives  16.3 us (22%)
  between operations  13.4 us (18%)
  local copies, waits for them, and re-layouts  2.65 us (4%)
  matrix products  1.69 us (2%)
  other arithmetic  0.9 us (1%)
    reduce_scatter x1, waiting for transfers between devices, shards(): lax.psum_scatter(lax.dot_general(masked, gathered, (((0,), (1,)), ((), ()...  39.7 us
    all_gather x1, blocking collectives, shards(): gathered = lax.all_gather(amplitudes, 'occ', axis=0, tiled=True)  16.3 us
    dot_general x1, matrix products, shards(): lax.dot_general(masked, gathered, (((0,), (1,)), ((), ())), preferred_ele...  1.69 us
  transfers between devices with their start and end apart: 1, of which 1 were waited for; matrix products, arithmetic and copies ran while one was open for 0% of the time, Pallas kernels for 0%

commit v1 on v0

v1 whole, which is shorter than its diff:
```python
import functools

import jax
import jax.numpy as jnp
from jax import lax
from jax.experimental import pallas as pl
from jax.experimental.pallas import tpu as pltpu
from jax.sharding import PartitionSpec as P

TILE = 128
ORDER = (3, 2, 1)
CHUNKS = ((0, 3, 2), (1,))


def prepare(chips, pos_ref, labels_ref, slots_ref, x_ref, keep_ref, send_ref):
    chip, core, vir, occ = pos_ref[0], pos_ref[1], pos_ref[2], pos_ref[3]
    slots = x_ref.shape[0] // TILE
    tiles = x_ref.shape[1] // TILE
    per = tiles // (2 * chips)
    for s in range(slots):
        rows = pl.ds(s * TILE, TILE)
        have = labels_ref[slots_ref[vir * slots + s]]
        for m in range(chips):
            for q in range(per):
                for out, c in ((keep_ref, core), (send_ref, 1 - core)):
                    t = ((chip ^ m) * 2 + c) * per + q
                    match = have == labels_ref[occ * tiles + t]
                    block = x_ref[rows, pl.ds(pl.multiple_of(t * TILE, TILE), TILE)]
                    out[rows, pl.ds((m * per + q) * TILE, TILE)] = jnp.where(
                        match, block, jnp.zeros_like(block)
                    )


def shards(nocc, nvir, amplitudes, integrals, labels, slot_tile):
    chips = nvir // 2
    vir = lax.axis_index("vir")
    occ = lax.axis_index("occ")
    chip, core = vir // 2, vir % 2
    depth, cols = integrals.shape
    width = cols // nvir
    rows = amplitudes.shape[0]

    def swap(x, axis, n, m):
        return lax.ppermute(x, axis, [(i, i ^ m) for i in range(n)])

    blocks = {0: amplitudes}
    for m in ORDER:
        blocks[m] = swap(amplitudes, "occ", nocc, m)
    pos = jnp.stack([chip, core, vir, occ]).astype(jnp.int32)
    half = jax.ShapeDtypeStruct((depth, cols // 2), integrals.dtype)
    smem = pl.BlockSpec(memory_space=pltpu.SMEM)
    vmem = pl.BlockSpec(memory_space=pltpu.VMEM)
    keep, send = pl.pallas_call(
        functools.partial(prepare, chips),
        out_shape=(half, half),
        in_specs=[smem, smem, smem, vmem],
        out_specs=(vmem, vmem),
    )(pos, labels, slot_tile, integrals)
    got = swap(send, "vir", nvir, 1)

    dot = functools.partial(jnp.dot, preferred_element_type=jnp.float32)
    out = jnp.zeros((nocc * rows, width), jnp.float32)
    for chunk in CHUNKS:
        parts = []
        for z in chunk:
            mine = blocks[z]
            other = swap(mine, "vir", nvir, 1)
            parts.append(dot(mine, keep) + dot(other, got))
        part = jnp.concatenate(parts, axis=0) if len(parts) > 1 else parts[0]
        total = part[:, :width]
        for m in range(1, chips):
            piece = part[:, m * width : (m + 1) * width].astype(jnp.float16)
            total = total + swap(piece, "vir", nvir, 2 * m).astype(jnp.float32)
        for n, z in enumerate(chunk):
            out = lax.dynamic_update_slice(out, total[n * rows : (n + 1) * rows], ((occ ^ z) * rows, 0))
    return out


def solution(mesh):
    in_specs = (P("occ", "vir"), P("vir", "occ"), P(), P())
    out_specs = P(None, ("occ", "vir"))
    f = functools.partial(shards, mesh.shape["occ"], mesh.shape["vir"])
    return jax.shard_map(f, mesh=mesh, in_specs=in_specs, out_specs=out_specs, check_vma=False)
```

time: 74.8 us -> 26.8 us (0.36)
  waiting for transfers between devices: 39.7 us -> 6.26 us
  blocking collectives: 16.3 us -> 0 us
  starting transfers between devices: 0.01 us -> 13.4 us
  between operations: 13.4 us -> 0.2 us
  Pallas kernels: 0 us -> 2.54 us
  local copies, waits for them, and re-layouts: 2.65 us -> 0.12 us
  matrix products: 1.69 us -> 2.79 us
    reduce_scatter x1 -> x0, waiting for transfers between devices: 39.7 us -> none  [shards(): lax.psum_scatter(lax.dot_general(masked, gathered, (((0,), (1,)), ((), ()...]
    all_gather x1 -> x0, blocking collectives: 16.3 us -> none  [shards(): gathered = lax.all_gather(amplitudes, 'occ', axis=0, tiled=True)]
    ppermute x0 -> x14, starting transfers between devices: none -> 13.4 us  [swap(): return lax.ppermute(x, axis, [(i, i ^ m) for i in range(n)])]
    ppermute x0 -> x14, waiting for transfers between devices: none -> 6.26 us  [swap(): return lax.ppermute(x, axis, [(i, i ^ m) for i in range(n)])]
    pallas_call x0 -> x1, Pallas kernels: none -> 2.54 us  [shards(): pl.pallas_call(functools.partial(prepare, chips), out_shape=(half, half),...]
    gather x1 -> x0, local copies, waits for them, and re-layouts: 1.29 us -> none  [shards(): slot_label = labels[my_slots]]
    dot_general x1 -> x8, matrix products: 1.69 us -> 2.79 us  [shards(): parts.append(dot(mine, keep) + dot(other, got))]
    select_n x1 -> x0, other arithmetic: 0.82 us -> none  [shards(): slot_label = labels[my_slots]]
  transfers between devices with their start and end apart: 1 -> 14, of which waited for: 1 -> 6; matrix products, arithmetic and copies ran while one was open for 0% -> 13% of each run, Pallas kernels for 0% -> 10%
where the time goes in v1:
time: 26.8 us; the launch traced here: 26.6 us
  starting transfers between devices  13.4 us (50%)
  waiting for transfers between devices  6.26 us (23%)
  matrix products  2.79 us (10%)
  Pallas kernels  2.54 us (9%)
  other arithmetic  1.3 us (5%)
    ppermute x14, starting transfers between devices, swap(): return lax.ppermute(x, axis, [(i, i ^ m) for i in range(n)])  13.4 us
    ppermute x14, waiting for transfers between devices, swap(): return lax.ppermute(x, axis, [(i, i ^ m) for i in range(n)])  6.26 us
    dot_general x8, matrix products, shards(): parts.append(dot(mine, keep) + dot(other, got))  2.79 us
    pallas_call x1, Pallas kernels, shards(): pl.pallas_call(functools.partial(prepare, chips), out_shape=(half, half),...  2.54 us
    dynamic_update_slice x1, other arithmetic, shards(): lax.dynamic_update_slice(out, total[n * rows:(n + 1) * rows], ((occ ^ z)...  0.64 us
    another operation x1, other arithmetic, shards(): pos = jnp.stack([chip, core, vir, occ]).astype(jnp.int32)  0.56 us
  transfers between devices with their start and end apart: 14, of which 6 were waited for; matrix products, arithmetic and copies ran while one was open for 13% of the time, Pallas kernels for 10%

profile of v1, /device:TPU:0, one launch (start us, length us, event | category | flops | bytes accessed | tf_op | source)
XLA Modules:
  0.0 26.6 jit_solution(8907432682909553970)
XLA Ops:
  0.0 5.1 %collective-permute-start.2 = (bf16[88,512]{1,0:T(8,128)(2,1)}, bf16[88,512]{1,0:T(8,128)(2,1)S(1)}, u32[]{:S(2)}, u32[]{:S(2)}) collective-permute-start(bf16[88,512]{1,0:T(8,128)(2,1)} %param.4), channel_id=1, source_target_pairs={{0,24},{8,16},{16,8},{24,0},{1,25},{9,17},{17,9},{25,1},{2,26},{10... | collective-permute-start | bytes 270344 | tf_op jit(solution)/shard_map/ppermute | solution.py:44
  5.1 0.0 collective-permute-start.1
  5.1 0.0 collective-permute-start.9
  5.1 0.6 %collective-permute-start.4 = (bf16[88,512]{1,0:T(8,128)(2,1)}, bf16[88,512]{1,0:T(8,128)(2,1)S(1)}, u32[]{:S(2)}, u32[]{:S(2)}) collective-permute-start(bf16[88,512]{1,0:T(8,128)(2,1)} %param.4), channel_id=1, source_target_pairs={{0,16},{8,24},{16,0},{24,8},{1,17},{9,25},{17,1},{25,9},{2,18},{10... | collective-permute-start | bytes 270344 | tf_op jit(solution)/shard_map/ppermute | solution.py:44
  5.7 0.6 %pad_add_fusion.pos_ref = s32[4]{0:T(128)} fusion(s32[1]{0:T(128)} %bitcast.3, s32[1]{0:T(128)} %bitcast.2, s32[1]{0:T(128)} %bitcast.1, s32[1]{0:T(128)} %bitcast), kind=kLoop, calls=%fused_computation.19 | loop fusion | flops 12 | bytes 32 | tf_op jit(solution)/shard_map/stack | solution.py:49
  6.3 0.0 copy-start.2
  6.3 2.5 %shard_map.46 = (bf16[512,512]{1,0:T(8,128)(2,1)}, bf16[512,512]{1,0:T(8,128)(2,1)}) custom-call(s32[4]{0:T(128)} %pad_add_fusion.pos_ref, s32[32]{0:T(128)} %labels_ref.1, s32[32]{0:T(128)} %slots_ref.1, bf16[512,1024]{1,0:T(8,128)(2,1)} %x_ref.1), custom_call_target="tpu_custom_call" | custom-call | tf_op jit(solution)/shard_map/pallas_call | solution.py:53
  8.8 0.0 copy-start
  8.8 0.0 collective-permute-start
  8.8 0.0 copy-done.2
  8.8 1.3 %fusion.13 = f32[512,88]{0,1:T(8,128)S(1)} fusion(bf16[512,512]{1,0:T(8,128)(2,1)} %get-tuple-element.7, bf16[88,512]{1,0:T(8,128)(2,1)S(1)} %copy-done.2), kind=kOutput, calls=%fused_computation.24 | convolution fusion | flops 46137344 | bytes 794624 | tf_op jit(solution)/shard_map/dot_general | solution.py:68
  10.2 1.5 %collective-permute-done.9 = bf16[88,512]{1,0:T(8,128)(2,1)S(1)} collective-permute-done((bf16[88,512]{1,0:T(8,128)(2,1)}, bf16[88,512]{1,0:T(8,128)(2,1)S(1)}, u32[]{:S(2)}, u32[]{:S(2)}) %collective-permute-start.9) | collective-permute-done | bytes 90144 | tf_op jit(solution)/shard_map/ppermute | solution.py:44
  11.7 0.0 collective-permute-start.10
  11.7 0.0 copy-done
  11.7 0.2 fusion.16
  11.9 0.0 collective-permute-done.2
  11.9 0.6 %collective-permute-start.3 = (bf16[88,512]{1,0:T(8,128)(2,1)S(1)}, bf16[88,512]{1,0:T(8,128)(2,1)S(1)}, u32[]{:S(2)}, u32[]{:S(2)}) collective-permute-start(bf16[88,512]{1,0:T(8,128)(2,1)S(1)} %collective-permute-done.2), channel_id=1, source_target_pairs={{0,1},{1,0},{2,3},{3,2},{4,5},{5,4},{6,7},{7,6},{8,9},{9,8},{10,11... | collective-permute-start | bytes 270344 | tf_op jit(solution)/shard_map/ppermute | solution.py:44
  12.5 0.7 %collective-permute-done.4 = bf16[88,512]{1,0:T(8,128)(2,1)S(1)} collective-permute-done((bf16[88,512]{1,0:T(8,128)(2,1)}, bf16[88,512]{1,0:T(8,128)(2,1)S(1)}, u32[]{:S(2)}, u32[]{:S(2)}) %collective-permute-start.4) | collective-permute-done | bytes 90144 | tf_op jit(solution)/shard_map/ppermute | solution.py:44
  13.2 0.0 collective-permute-start.5
  13.2 0.2 fusion.15
  13.4 0.2 fusion.14
  13.6 0.9 %collective-permute-done.5 = bf16[88,512]{1,0:T(8,128)(2,1)S(1)} collective-permute-done((bf16[88,512]{1,0:T(8,128)(2,1)S(1)}, bf16[88,512]{1,0:T(8,128)(2,1)S(1)}, u32[]{:S(2)}, u32[]{:S(2)}) %collective-permute-start.5) | collective-permute-done | bytes 90144 | tf_op jit(solution)/shard_map/ppermute | solution.py:44
  14.5 0.0 collective-permute-done
  14.5 0.2 fusion.1
  14.7 0.0 collective-permute-done.3
  14.7 0.2 fusion.2
  14.9 0.0 collective-permute-done.1
  15.0 0.2 fusion.3
  15.2 0.1 fusion.9
  15.3 1.6 %collective-permute-start.6 = (f16[264,128]{1,0:T(8,128)(2,1)S(1)}, f16[264,128]{1,0:T(8,128)(2,1)S(1)}, u32[]{:S(2)}, u32[]{:S(2)}) collective-permute-start(f16[264,128]{1,0:T(8,128)(2,1)S(1)} %get-tuple-element.11), channel_id=1, source_target_pairs={{0,2},{1,3},{2,0},{3,1},{4,6},{5,7},{6,4},{7,5},{8,10},{9,11},{10,... | collective-permute-start | bytes 202760 | tf_op jit(solution)/shard_map/ppermute | solution.py:44
  16.9 1.5 %collective-permute-start.8 = (f16[264,128]{1,0:T(8,128)(2,1)S(1)}, f16[264,128]{1,0:T(8,128)(2,1)S(1)}, u32[]{:S(2)}, u32[]{:S(2)}) collective-permute-start(f16[264,128]{1,0:T(8,128)(2,1)S(1)} %get-tuple-element.12), channel_id=1, source_target_pairs={{0,6},{1,7},{2,4},{3,5},{4,2},{5,3},{6,0},{7,1},{8,14},{9,15},{10,... | collective-permute-start | bytes 202760 | tf_op jit(solution)/shard_map/ppermute | solution.py:44
  18.4 0.5 %collective-permute-start.7 = (f16[264,128]{1,0:T(8,128)(2,1)S(1)}, f16[264,128]{1,0:T(8,128)(2,1)S(1)}, u32[]{:S(2)}, u32[]{:S(2)}) collective-permute-start(f16[264,128]{1,0:T(8,128)(2,1)S(1)} %get-tuple-element.13), channel_id=1, source_target_pairs={{0,4},{1,5},{2,6},{3,7},{4,0},{5,1},{6,2},{7,3},{8,12},{9,13},{10,... | collective-permute-start | bytes 202760 | tf_op jit(solution)/shard_map/ppermute | solution.py:44
  18.9 0.0 collective-permute-done.10
  18.9 0.2 fusion.12
  19.1 1.6 %collective-permute-start.11 = (f16[88,128]{1,0:T(8,128)(2,1)S(1)}, f16[88,128]{1,0:T(8,128)(2,1)S(1)}, u32[]{:S(2)}, u32[]{:S(2)}) collective-permute-start(f16[88,128]{1,0:T(8,128)(2,1)S(1)} %get-tuple-element.14), channel_id=1, source_target_pairs={{0,2},{1,3},{2,0},{3,1},{4,6},{5,7},{6,4},{7,5},{8,10},{9,11},{10,... | collective-permute-start | bytes 67592 | tf_op jit(solution)/shard_map/ppermute | solution.py:44
  20.7 1.5 %collective-permute-start.13 = (f16[88,128]{1,0:T(8,128)(2,1)S(1)}, f16[88,128]{1,0:T(8,128)(2,1)S(1)}, u32[]{:S(2)}, u32[]{:S(2)}) collective-permute-start(f16[88,128]{1,0:T(8,128)(2,1)S(1)} %get-tuple-element.15), channel_id=1, source_target_pairs={{0,6},{1,7},{2,4},{3,5},{4,2},{5,3},{6,0},{7,1},{8,14},{9,15},{10,... | collective-permute-start | bytes 67592 | tf_op jit(solution)/shard_map/ppermute | solution.py:44
  22.2 0.0 collective-permute-done.6
  22.2 0.5 %collective-permute-start.12 = (f16[88,128]{1,0:T(8,128)(2,1)S(1)}, f16[88,128]{1,0:T(8,128)(2,1)S(1)}, u32[]{:S(2)}, u32[]{:S(2)}) collective-permute-start(f16[88,128]{1,0:T(8,128)(2,1)S(1)} %get-tuple-element.16), channel_id=1, source_target_pairs={{0,4},{1,5},{2,6},{3,7},{4,0},{5,1},{6,2},{7,3},{8,12},{9,13},{10,... | collective-permute-start | bytes 67592 | tf_op jit(solution)/shard_map/ppermute | solution.py:44
  22.7 0.0 collective-permute-done.8
  22.7 0.6 %collective-permute-done.7 = f16[264,128]{1,0:T(8,128)(2,1)S(1)} collective-permute-done((f16[264,128]{1,0:T(8,128)(2,1)S(1)}, f16[264,128]{1,0:T(8,128)(2,1)S(1)}, u32[]{:S(2)}, u32[]{:S(2)}) %collective-permute-start.7) | collective-permute-done | bytes 67616 | tf_op jit(solution)/shard_map/ppermute | solution.py:44
  23.4 0.0 copy-start.1
  23.4 0.0 collective-permute-done.11
  23.4 1.9 %collective-permute-done.13 = f16[88,128]{1,0:T(8,128)(2,1)S(1)} collective-permute-done((f16[88,128]{1,0:T(8,128)(2,1)S(1)}, f16[88,128]{1,0:T(8,128)(2,1)S(1)}, u32[]{:S(2)}, u32[]{:S(2)}) %collective-permute-start.13) | collective-permute-done | bytes 22560 | tf_op jit(solution)/shard_map/ppermute | solution.py:44
  25.4 0.6 %collective-permute-done.12 = f16[88,128]{1,0:T(8,128)(2,1)S(1)} collective-permute-done((f16[88,128]{1,0:T(8,128)(2,1)S(1)}, f16[88,128]{1,0:T(8,128)(2,1)S(1)}, u32[]{:S(2)}, u32[]{:S(2)}) %collective-permute-start.12) | collective-permute-done | bytes 22560 | tf_op jit(solution)/shard_map/ppermute | solution.py:44
  26.0 0.0 copy-done.1
  26.0 0.6 %fusion.8 = f32[352,128]{1,0:T(8,128)} fusion(f32[352,128]{1,0:T(8,128)} %copy-done.1, s32[]{:T(128)S(6)} %select_n.28, f32[88,512]{1,0:T(8,128)S(1)} %get-tuple-element.18, f16[88,128]{1,0:T(8,128)(2,1)S(1)} %collective-permute-done.13, f16[88,128]{1,0:T(8,128)(2,1)S(1)} %collective-permute-done.12, f16[88,128]{1,0:T(8,128)(2,1)S(1)} %collective-permute-done.11), kind=kLoop, calls=%fused_computation.15 | loop fusion | flops 67584 | bytes 157700 | tf_op jit(solution)/shard_map/dynamic_update_slice | solution.py:75
  (7 shorter events, 0.1 us)
Async XLA Ops:
  0.0 11.9 %collective-permute-start.2 = (bf16[88,512]{1,0:T(8,128)(2,1)}, bf16[88,512]{1,0:T(8,128)(2,1)S(1)}, u32[]{:S(2)}, u32[]{:S(2)}) collective-permute-start(bf16[88,512]{1,0:T(8,128)(2,1)} %param.4), channel_id=1, source_target_pairs={{0,24},{8,16},{16,8},{24,0},{1,25},{9,17},{17,9},{25,1},{2,26},{10... | collective-permute-start | bytes 270344 | tf_op jit(solution)/shard_map/ppermute | solution.py:44
  5.1 9.9 %collective-permute-start.1 = (bf16[88,512]{1,0:T(8,128)(2,1)}, bf16[88,512]{1,0:T(8,128)(2,1)S(1)}, u32[]{:S(2)}, u32[]{:S(2)}) collective-permute-start(bf16[88,512]{1,0:T(8,128)(2,1)} %param.4), channel_id=1, source_target_pairs={{0,1},{1,0},{2,3},{3,2},{4,5},{5,4},{6,7},{7,6},{8,9},{9,8},{10,11... | collective-permute-start | bytes 270344 | tf_op jit(solution)/shard_map/ppermute | solution.py:44
  5.1 6.6 %collective-permute-start.9 = (bf16[88,512]{1,0:T(8,128)(2,1)}, bf16[88,512]{1,0:T(8,128)(2,1)S(1)}, u32[]{:S(2)}, u32[]{:S(2)}) collective-permute-start(bf16[88,512]{1,0:T(8,128)(2,1)} %param.4), channel_id=1, source_target_pairs={{0,8},{8,0},{16,24},{24,16},{1,9},{9,1},{17,25},{25,17},{2,10},{10... | collective-permute-start | bytes 270344 | tf_op jit(solution)/shard_map/ppermute | solution.py:44
  5.1 8.1 %collective-permute-start.4 = (bf16[88,512]{1,0:T(8,128)(2,1)}, bf16[88,512]{1,0:T(8,128)(2,1)S(1)}, u32[]{:S(2)}, u32[]{:S(2)}) collective-permute-start(bf16[88,512]{1,0:T(8,128)(2,1)} %param.4), channel_id=1, source_target_pairs={{0,16},{8,24},{16,0},{24,8},{1,17},{9,25},{17,1},{25,9},{2,18},{10... | collective-permute-start | bytes 270344 | tf_op jit(solution)/shard_map/ppermute | solution.py:44
  6.3 2.5 %copy-start.2 = (bf16[88,512]{1,0:T(8,128)(2,1)S(1)}, bf16[88,512]{1,0:T(8,128)(2,1)}, u32[]{:S(2)}) copy-start(bf16[88,512]{1,0:T(8,128)(2,1)} %param.4) | copy-start | bytes 270340
  8.8 2.9 %copy-start = (bf16[512,512]{1,0:T(8,128)(2,1)S(1)}, bf16[512,512]{1,0:T(8,128)(2,1)}, u32[]{:S(2)}) copy-start(bf16[512,512]{1,0:T(8,128)(2,1)} %get-tuple-element.7) | copy-start | bytes 1572868
  8.8 5.7 %collective-permute-start = (bf16[512,512]{1,0:T(8,128)(2,1)}, bf16[512,512]{1,0:T(8,128)(2,1)S(1)}, u32[]{:S(2)}, u32[]{:S(2)}) collective-permute-start(bf16[512,512]{1,0:T(8,128)(2,1)} %get-tuple-element.8), channel_id=1, source_target_pairs={{0,1},{1,0},{2,3},{3,2},{4,5},{5,4},{6,7},{7,6},{8,9},{9,8},{10,11... | collective-permute-start | bytes 1572872 | tf_op jit(solution)/shard_map/ppermute | solution.py:44
  11.7 7.2 %collective-permute-start.10 = (bf16[88,512]{1,0:T(8,128)(2,1)S(1)}, bf16[88,512]{1,0:T(8,128)(2,1)S(1)}, u32[]{:S(2)}, u32[]{:S(2)}) collective-permute-start(bf16[88,512]{1,0:T(8,128)(2,1)S(1)} %collective-permute-done.9), channel_id=1, source_target_pairs={{0,1},{1,0},{2,3},{3,2},{4,5},{5,4},{6,7},{7,6},{8,9},{9,8},{10,11... | collective-permute-start | bytes 270344 | tf_op jit(solution)/shard_map/ppermute | solution.py:44
  11.9 2.8 %collective-permute-start.3 = (bf16[88,512]{1,0:T(8,128)(2,1)S(1)}, bf16[88,512]{1,0:T(8,128)(2,1)S(1)}, u32[]{:S(2)}, u32[]{:S(2)}) collective-permute-start(bf16[88,512]{1,0:T(8,128)(2,1)S(1)} %collective-permute-done.2), channel_id=1, source_target_pairs={{0,1},{1,0},{2,3},{3,2},{4,5},{5,4},{6,7},{7,6},{8,9},{9,8},{10,11... | collective-permute-start | bytes 270344 | tf_op jit(solution)/shard_map/ppermute | solution.py:44
  13.2 1.3 %collective-permute-start.5 = (bf16[88,512]{1,0:T(8,128)(2,1)S(1)}, bf16[88,512]{1,0:T(8,128)(2,1)S(1)}, u32[]{:S(2)}, u32[]{:S(2)}) collective-permute-start(bf16[88,512]{1,0:T(8,128)(2,1)S(1)} %collective-permute-done.4), channel_id=1, source_target_pairs={{0,1},{1,0},{2,3},{3,2},{4,5},{5,4},{6,7},{7,6},{8,9},{9,8},{10,11... | collective-permute-start | bytes 270344 | tf_op jit(solution)/shard_map/ppermute | solution.py:44
  15.3 6.9 %collective-permute-start.6 = (f16[264,128]{1,0:T(8,128)(2,1)S(1)}, f16[264,128]{1,0:T(8,128)(2,1)S(1)}, u32[]{:S(2)}, u32[]{:S(2)}) collective-permute-start(f16[264,128]{1,0:T(8,128)(2,1)S(1)} %get-tuple-element.11), channel_id=1, source_target_pairs={{0,2},{1,3},{2,0},{3,1},{4,6},{5,7},{6,4},{7,5},{8,10},{9,11},{10,... | collective-permute-start | bytes 202760 | tf_op jit(solution)/shard_map/ppermute | solution.py:44
  16.9 5.8 %collective-permute-start.8 = (f16[264,128]{1,0:T(8,128)(2,1)S(1)}, f16[264,128]{1,0:T(8,128)(2,1)S(1)}, u32[]{:S(2)}, u32[]{:S(2)}) collective-permute-start(f16[264,128]{1,0:T(8,128)(2,1)S(1)} %get-tuple-element.12), channel_id=1, source_target_pairs={{0,6},{1,7},{2,4},{3,5},{4,2},{5,3},{6,0},{7,1},{8,14},{9,15},{10,... | collective-permute-start | bytes 202760 | tf_op jit(solution)/shard_map/ppermute | solution.py:44
  18.4 4.9 %collective-permute-start.7 = (f16[264,128]{1,0:T(8,128)(2,1)S(1)}, f16[264,128]{1,0:T(8,128)(2,1)S(1)}, u32[]{:S(2)}, u32[]{:S(2)}) collective-permute-start(f16[264,128]{1,0:T(8,128)(2,1)S(1)} %get-tuple-element.13), channel_id=1, source_target_pairs={{0,4},{1,5},{2,6},{3,7},{4,0},{5,1},{6,2},{7,3},{8,12},{9,13},{10,... | collective-permute-start | bytes 202760 | tf_op jit(solution)/shard_map/ppermute | solution.py:44
  19.1 4.3 %collective-permute-start.11 = (f16[88,128]{1,0:T(8,128)(2,1)S(1)}, f16[88,128]{1,0:T(8,128)(2,1)S(1)}, u32[]{:S(2)}, u32[]{:S(2)}) collective-permute-start(f16[88,128]{1,0:T(8,128)(2,1)S(1)} %get-tuple-element.14), channel_id=1, source_target_pairs={{0,2},{1,3},{2,0},{3,1},{4,6},{5,7},{6,4},{7,5},{8,10},{9,11},{10,... | collective-permute-start | bytes 67592 | tf_op jit(solution)/shard_map/ppermute | solution.py:44
  20.7 4.7 %collective-permute-start.13 = (f16[88,128]{1,0:T(8,128)(2,1)S(1)}, f16[88,128]{1,0:T(8,128)(2,1)S(1)}, u32[]{:S(2)}, u32[]{:S(2)}) collective-permute-start(f16[88,128]{1,0:T(8,128)(2,1)S(1)} %get-tuple-element.15), channel_id=1, source_target_pairs={{0,6},{1,7},{2,4},{3,5},{4,2},{5,3},{6,0},{7,1},{8,14},{9,15},{10,... | collective-permute-start | bytes 67592 | tf_op jit(solution)/shard_map/ppermute | solution.py:44
  22.2 3.8 %collective-permute-start.12 = (f16[88,128]{1,0:T(8,128)(2,1)S(1)}, f16[88,128]{1,0:T(8,128)(2,1)S(1)}, u32[]{:S(2)}, u32[]{:S(2)}) collective-permute-start(f16[88,128]{1,0:T(8,128)(2,1)S(1)} %get-tuple-element.16), channel_id=1, source_target_pairs={{0,4},{1,5},{2,6},{3,7},{4,0},{5,1},{6,2},{7,3},{8,12},{9,13},{10,... | collective-permute-start | bytes 67592 | tf_op jit(solution)/shard_map/ppermute | solution.py:44
  23.4 2.6 %copy-start.1 = (f32[352,128]{1,0:T(8,128)}, f32[352,128]{1,0:T(8,128)S(1)}, u32[]{:S(2)}) copy-start(f32[352,128]{1,0:T(8,128)S(1)} %slice_dynamic-update-slice_fusion) | copy-start | bytes 540676
